TPU v7x, 256 devices: a whole 4x4x8 slice. The times are simulated.
256 devices in a mesh: gx: 8 (over z_lo, y), gy: 8 (over x, core), dir: 4 (over z_hi).
Axes of the slice: x: 4, y: 4, z: 8 (z_hi: 4, z_lo: 2; z = z_hi * 2 + z_lo), core: 2. Of those that a mesh axis runs over, the one named last changes fastest.
Arguments:
- directions: float32 [32, 1024, 2048], P('dir', 'gx', 'gy'), may hold values from -6 to 6
- velocity: float32 [2, 1024, 2048], P(None, 'gx', 'gy'), may hold values from -6 to 6
- viscosity: float32 [1024, 2048], P('gx', 'gy'), may hold values from 0.5 to 2
- basal_drag: float32 [1024, 2048], P('gx', 'gy'), may hold values from 0.5 to 8
- misfit_weight: float32 [1024, 2048], P('gx', 'gy'), may hold values from 1 to 10
- ice_mask: int32 [1024, 2048], P('gx', 'gy'), may hold values 0 or 1
- grounded: int32 [1024, 2048], P('gx', 'gy'), may hold values 0 or 1
Outputs:
- basis: float32 [32, 1024, 2048], P('dir', 'gx', 'gy')
- upper: float32 [32, 32], replicated
All inputs are finite; a program needn't handle non-finite values. No bound on the sum of `ice_mask` or of `grounded` on one device may be relied on, other than what follows from the above.
Results may differ from a plain program's by a relative error of at most 0.00021.
Values sent between devices are 32-bit elements; how exact they have to be, the bound alone decides.
A program may use at most 64 MiB of HBM per device.

v0:
```python
import jax
import jax.numpy as jnp
from jax import lax
from jax.sharding import PartitionSpec as P

SWEEPS = 6
damping = 0.8


def with_halo(value, sides, width):
    for axis, dim in sides:
        count, length = (lax.axis_size(axis), value.shape[dim])
        up = [(i, (i + 1) % count) for i in range(count - 1)]
        down = [(j, i) for i, j in up]
        last = lax.slice_in_dim(value, length - width, length, axis=dim)
        first = lax.slice_in_dim(value, 0, width, axis=dim)
        before = lax.ppermute(last, axis, up)
        after = lax.ppermute(first, axis, down)
        value = jnp.concatenate([before, value, after], axis=dim)
    return value


def weights_pair():
    along_x = jnp.array([4.0, 1.0], jnp.float32).reshape(2, 1, 1)
    along_y = jnp.array([1.0, 4.0], jnp.float32).reshape(2, 1, 1)
    return (along_x, along_y)


def relax_sweep(state, padded, coeffs, source):
    face_east, face_west, face_north, face_south, friction, diagonal, ice_keep = coeffs
    along_x, along_y = weights_pair()
    next_row = padded[..., 2:, 1:-1]
    prev_row = padded[..., :-2, 1:-1]
    next_col = padded[..., 1:-1, 2:]
    prev_col = padded[..., 1:-1, :-2]
    applied = along_x * (face_east * (state - next_row) + face_west * (state - prev_row))
    applied = applied + along_y * (
        face_north * (state - next_col) + face_south * (state - prev_col)
    )
    applied = applied + friction * state
    return ice_keep * (state + damping * (source - applied) / diagonal)


def solve_shared(source, coeffs):
    diagonal, ice_keep = (coeffs[5], coeffs[6])
    state = ice_keep * damping * source / diagonal
    for sweep in range(SWEEPS - 1):
        padded = with_halo(state, (("gx", 2), ("gy", 3)), 1)
        state = relax_sweep(state, padded, coeffs, source)
    return state


def make_coeffs(viscosity, padded_visc, basal_drag, grounded_f):
    face_east = 0.5 * (viscosity + padded_visc[2:, 1:-1])
    face_west = 0.5 * (viscosity + padded_visc[:-2, 1:-1])
    face_north = 0.5 * (viscosity + padded_visc[1:-1, 2:])
    face_south = 0.5 * (viscosity + padded_visc[1:-1, :-2])
    friction = basal_drag * grounded_f
    along_x, along_y = weights_pair()
    diagonal = along_x * (face_east + face_west) + along_y * (face_north + face_south) + friction
    return (face_east, face_west, face_north, face_south, friction, diagonal)


def on_device(directions, velocity, viscosity, basal_drag, misfit_weight, ice_mask, grounded):
    own_count = directions.shape[0]
    tile_rows = directions.shape[1]
    tile_cols = directions.shape[2]
    padded_visc = with_halo(viscosity, (("gx", 0), ("gy", 1)), 1)
    ice_keep = ice_mask.astype(jnp.float32)
    face_east, face_west, face_north, face_south, friction, diagonal = make_coeffs(
        viscosity, padded_visc, basal_drag, grounded.astype(jnp.float32)
    )
    coeffs = (face_east, face_west, face_north, face_south, friction, diagonal, ice_keep)
    forward = solve_shared(-friction * velocity[None] * directions[:, None], coeffs)
    adjoint = solve_shared(misfit_weight * forward, coeffs)
    sketch = -friction * jnp.sum(velocity[None] * adjoint, axis=1)
    cells = tile_rows * tile_cols
    total_cells = cells * lax.axis_size("gx") * lax.axis_size("gy")
    own_flat = sketch.reshape(own_count, cells)
    identity = jnp.eye(own_count * lax.axis_size("dir"), dtype=jnp.float32)
    whole = lax.all_gather(own_flat, "dir", axis=0, tiled=True)
    gram_local = jnp.dot(
        whole, whole.T, precision=lax.Precision.HIGHEST, preferred_element_type=jnp.float32
    )
    gram_sum = lax.psum(gram_local, ("gx", "gy"))
    lower = jnp.linalg.cholesky(gram_sum / jnp.float32(total_cells))
    inverse = lax.linalg.triangular_solve(lower, identity, left_side=True, lower=True)
    own_rows = lax.dynamic_slice_in_dim(inverse, lax.axis_index("dir") * own_count, own_count, 0)
    basis_flat = jnp.dot(
        own_rows, whole, precision=lax.Precision.HIGHEST, preferred_element_type=jnp.float32
    )
    return (basis_flat.reshape(own_count, tile_rows, tile_cols), lower.T)


def solution(mesh):
    placed = (
        P("dir", "gx", "gy"),
        P(None, "gx", "gy"),
        P("gx", "gy"),
        P("gx", "gy"),
        P("gx", "gy"),
        P("gx", "gy"),
        P("gx", "gy"),
    )
    return jax.shard_map(
        on_device,
        mesh=mesh,
        in_specs=placed,
        out_specs=(P("dir", "gx", "gy"), P()),
        check_vma=False,
    )
```

profile of v0, /device:TPU:64, one launch (start us, length us, event | category | flops | bytes accessed | tf_op | source)
XLA Modules:
  0.0 741.2 jit_solution(18365183644680429997)
XLA Ops:
  9.3 4.5 collective-permute-start.1
  17.9 3.0 collective-permute-start.3
  25.3 4.5 collective-permute-start.5
  37.2 3.0 collective-permute-start.7
  44.3 7.2 fusion.4
  52.8 5.0 collective-permute-start.9
  61.5 2.5 copy.104
  65.2 2.5 copy.106
  67.7 4.8 collective-permute-start.11
  77.2 5.3 fusion.8
  83.9 4.8 collective-permute-start.13
  92.3 2.6 copy.108
  96.3 2.5 copy.110
  98.7 4.1 collective-permute-start.15
  102.9 2.4 copy.109
  107.6 5.3 fusion.12
  114.2 6.7 collective-permute-start.17
  124.6 2.6 copy.112
  128.5 2.5 copy.114
  131.0 3.6 collective-permute-start.19
  134.6 2.4 copy.113
  139.4 5.3 fusion.16
  146.0 6.9 collective-permute-start.21
  160.3 3.0 collective-permute-start.23
  166.7 8.1 %multiply_divide_fusion = (f32[8,2,128,256]{3,0,2,1:T(8,128)S(1)}, f32[8,2,128,256]{3,0,2,1:T(8,128)S(1)}) fusion(f32[2,128,256]{2,1,0:T(8,128)S(1)} %get-tuple-element.69, f32[128,256]{1,0:T(8,128)} %copy-done.17, f32[8,2,128,256]{3,0,2,1:T(8,128)} %copy-done.9, f32[128,256]{1,0:T(8,128)S(1)} %get-tuple-element.11, ...), kind=kLoop, calls=%fused_computation.279 | loop fusion | flops 16777216 | bytes 8962320 | tf_op jit(solution)/shard_map/div | solution.py:46
  176.1 6.7 collective-permute-start.25
  191.3 3.6 collective-permute-start.27
  198.2 7.3 fusion.182
  206.9 6.9 collective-permute-start.29
  222.2 4.0 collective-permute-start.31
  229.5 7.0 fusion.183
  237.8 6.7 collective-permute-start.33
  252.8 3.8 collective-permute-start.35
  260.0 7.0 fusion.184
  268.3 6.9 collective-permute-start.37
  283.8 4.0 collective-permute-start.39
  291.2 7.0 fusion.185
  299.5 6.9 collective-permute-start.41
  310.1 2.5 copy.136
  313.9 2.5 copy.138
  316.4 4.6 collective-permute-start.43
  326.7 7.1 multiply_reduce_fusion
  335.0 99.5 %all-gather.2.cloned.1.call-done = f32[32,32768]{1,0:T(8,128)} async-done(((f32[8,32768]{1,0:T(8,128)}), f32[32,32768]{1,0:T(8,128)}) %all-gather.2.cloned.1.call-update) | async-done | bytes 4194320 | tf_op jit(solution)/shard_map/all_gather | solution.py:81
  434.4 6.9 fusion.230
  441.4 279.7 %psum.7 = f32[32,32]{0,1:T(8,128)S(1)} all-reduce(f32[32,32]{0,1:T(8,128)S(1)} %fusion.230), channel_id=1, replica_groups=mesh['gx'=8,'gy'=8,'dir'=4] {'gx','gy'}, use_global_device_ids=true, to_apply=%region_1.0 | all-reduce | flops 1024 | bytes 8192 | tf_op jit(solution)/shard_map/psum | solution.py:85
  721.2 2.9 cholesky.17
  725.4 2.4 custom-call.6
  728.1 3.8 fusion.198
  (216 shorter events, 130.6 us)
Async XLA Ops:
  7.2 15.4 %copy-start.21 = (f32[128,256]{1,0:T(8,128)S(1)}, f32[128,256]{1,0:T(8,128)}, u32[]{:S(2)}) copy-start(f32[128,256]{1,0:T(8,128)} %param.31) | copy-start | bytes 393220
  7.2 427.3 %all-gather.2.cloned.1.call-start = ((), (), s32[]{:S(2)}) async-start(), calls=%async_computation | async-start | bytes 5242880 | tf_op jit(solution)/shard_map/all_gather | solution.py:81
  8.0 7.5 %collective-permute-start = (f32[1,256]{1,0:T(1,128)S(1)}, f32[1,256]{1,0:T(1,128)S(1)}, u32[]{:S(2)}, u32[]{:S(2)}) collective-permute-start(f32[1,256]{1,0:T(1,128)S(1)} %get-tuple-element.66), channel_id=1, source_target_pairs={{32,0},{64,32},{96,64},{128,96},{160,128},{192,160},{224,192},{33,... | collective-permute-start | bytes 3080 | tf_op jit(solution)/shard_map/ppermute | solution.py:18
  9.3 6.2 collective-permute-start.1
  16.6 5.9 collective-permute-start.2
  17.9 4.6 collective-permute-start.3
  24.0 5.9 collective-permute-start.4
  25.3 6.0 collective-permute-start.5
  35.3 5.7 collective-permute-start.6
  37.2 5.4 collective-permute-start.7
  51.5 6.3 collective-permute-start.8
  52.8 6.4 collective-permute-start.9
  64.0 8.6 %collective-permute-start.10 = (f32[8,2,130,1]{2,0,3,1:T(8,128)}, f32[8,2,130,1]{2,0,3,1:T(8,128)}, u32[]{:S(2)}, u32[]{:S(2)}) collective-permute-start(f32[8,2,130,1]{2,0,3,1:T(8,128)} %copy.104), channel_id=1, source_target_pairs={{4,0},{8,4},{12,8},{16,12},{20,16},{24,20},{28,24},{5,1},{9,5},{13... | collective-permute-start | bytes 24968 | tf_op jit(solution)/shard_map/ppermute | solution.py:18
  67.7 7.2 collective-permute-start.11
  82.6 6.1 collective-permute-start.12
  83.9 6.2 collective-permute-start.13
  92.3 15.3 %copy-start.2 = (f32[8,2,128,256]{3,0,2,1:T(8,128)S(1)}, f32[8,2,128,256]{3,0,2,1:T(8,128)}, u32[]{:S(2)}) copy-start(f32[8,2,128,256]{3,0,2,1:T(8,128)} %copy-done.1) | copy-start | bytes 6291460
  95.0 7.9 %collective-permute-start.14 = (f32[8,2,130,1]{2,0,3,1:T(8,128)}, f32[8,2,130,1]{2,0,3,1:T(8,128)}, u32[]{:S(2)}, u32[]{:S(2)}) collective-permute-start(f32[8,2,130,1]{2,0,3,1:T(8,128)} %copy.108), channel_id=1, source_target_pairs={{4,0},{8,4},{12,8},{16,12},{20,16},{24,20},{28,24},{5,1},{9,5},{13... | collective-permute-start | bytes 24968 | tf_op jit(solution)/shard_map/ppermute | solution.py:18
  98.7 6.5 collective-permute-start.15
  112.9 8.0 %collective-permute-start.16 = (f32[8,2,1,256]{3,0,2,1:T(8,128)S(1)}, f32[8,2,1,256]{3,0,2,1:T(8,128)S(1)}, u32[]{:S(2)}, u32[]{:S(2)}) collective-permute-start(f32[8,2,1,256]{3,0,2,1:T(8,128)S(1)} %get-tuple-element.53), channel_id=1, source_target_pairs={{32,0},{64,32},{96,64},{128,96},{160,128},{192,160},{224,192},{33,... | collective-permute-start | bytes 49160 | tf_op jit(solution)/shard_map/ppermute | solution.py:18
  114.2 8.1 %collective-permute-start.17 = (f32[8,2,1,256]{3,0,2,1:T(8,128)S(1)}, f32[8,2,1,256]{3,0,2,1:T(8,128)S(1)}, u32[]{:S(2)}, u32[]{:S(2)}) collective-permute-start(f32[8,2,1,256]{3,0,2,1:T(8,128)S(1)} %get-tuple-element.52), channel_id=1, source_target_pairs={{0,32},{32,64},{64,96},{96,128},{128,160},{160,192},{192,224},{1,3... | collective-permute-start | bytes 49160 | tf_op jit(solution)/shard_map/ppermute | solution.py:17
  127.2 7.4 collective-permute-start.18
  131.0 6.0 collective-permute-start.19
  144.7 8.2 %collective-permute-start.20 = (f32[8,2,1,256]{3,0,2,1:T(8,128)S(1)}, f32[8,2,1,256]{3,0,2,1:T(8,128)S(1)}, u32[]{:S(2)}, u32[]{:S(2)}) collective-permute-start(f32[8,2,1,256]{3,0,2,1:T(8,128)S(1)} %get-tuple-element.51), channel_id=1, source_target_pairs={{32,0},{64,32},{96,64},{128,96},{160,128},{192,160},{224,192},{33,... | collective-permute-start | bytes 49160 | tf_op jit(solution)/shard_map/ppermute | solution.py:18
  146.0 8.4 %collective-permute-start.21 = (f32[8,2,1,256]{3,0,2,1:T(8,128)S(1)}, f32[8,2,1,256]{3,0,2,1:T(8,128)S(1)}, u32[]{:S(2)}, u32[]{:S(2)}) collective-permute-start(f32[8,2,1,256]{3,0,2,1:T(8,128)S(1)} %get-tuple-element.50), channel_id=1, source_target_pairs={{0,32},{32,64},{64,96},{96,128},{128,160},{160,192},{192,224},{1,3... | collective-permute-start | bytes 49160 | tf_op jit(solution)/shard_map/ppermute | solution.py:17
  158.3 5.0 collective-permute-start.22
  160.3 4.7 collective-permute-start.23
  174.8 8.0 %collective-permute-start.24 = (f32[8,2,1,256]{3,0,2,1:T(8,128)S(1)}, f32[8,2,1,256]{3,0,2,1:T(8,128)S(1)}, u32[]{:S(2)}, u32[]{:S(2)}) collective-permute-start(f32[8,2,1,256]{3,0,2,1:T(8,128)S(1)} %get-tuple-element.49), channel_id=1, source_target_pairs={{32,0},{64,32},{96,64},{128,96},{160,128},{192,160},{224,192},{33,... | collective-permute-start | bytes 49160 | tf_op jit(solution)/shard_map/ppermute | solution.py:18
  176.1 8.1 %collective-permute-start.25 = (f32[8,2,1,256]{3,0,2,1:T(8,128)S(1)}, f32[8,2,1,256]{3,0,2,1:T(8,128)S(1)}, u32[]{:S(2)}, u32[]{:S(2)}) collective-permute-start(f32[8,2,1,256]{3,0,2,1:T(8,128)S(1)} %get-tuple-element.48), channel_id=1, source_target_pairs={{0,32},{32,64},{64,96},{96,128},{128,160},{160,192},{192,224},{1,3... | collective-permute-start | bytes 49160 | tf_op jit(solution)/shard_map/ppermute | solution.py:17
  188.1 6.8 collective-permute-start.26
  191.3 5.3 collective-permute-start.27
  205.6 8.2 %collective-permute-start.28 = (f32[8,2,1,256]{3,0,2,1:T(8,128)S(1)}, f32[8,2,1,256]{3,0,2,1:T(8,128)S(1)}, u32[]{:S(2)}, u32[]{:S(2)}) collective-permute-start(f32[8,2,1,256]{3,0,2,1:T(8,128)S(1)} %get-tuple-element.47), channel_id=1, source_target_pairs={{32,0},{64,32},{96,64},{128,96},{160,128},{192,160},{224,192},{33,... | collective-permute-start | bytes 49160 | tf_op jit(solution)/shard_map/ppermute | solution.py:18
  206.9 8.4 %collective-permute-start.29 = (f32[8,2,1,256]{3,0,2,1:T(8,128)S(1)}, f32[8,2,1,256]{3,0,2,1:T(8,128)S(1)}, u32[]{:S(2)}, u32[]{:S(2)}) collective-permute-start(f32[8,2,1,256]{3,0,2,1:T(8,128)S(1)} %get-tuple-element.46), channel_id=1, source_target_pairs={{0,32},{32,64},{64,96},{96,128},{128,160},{160,192},{192,224},{1,3... | collective-permute-start | bytes 49160 | tf_op jit(solution)/shard_map/ppermute | solution.py:17
  219.0 7.2 collective-permute-start.30
  222.2 5.7 collective-permute-start.31
  236.6 8.0 %collective-permute-start.32 = (f32[8,2,1,256]{3,0,2,1:T(8,128)S(1)}, f32[8,2,1,256]{3,0,2,1:T(8,128)S(1)}, u32[]{:S(2)}, u32[]{:S(2)}) collective-permute-start(f32[8,2,1,256]{3,0,2,1:T(8,128)S(1)} %get-tuple-element.45), channel_id=1, source_target_pairs={{32,0},{64,32},{96,64},{128,96},{160,128},{192,160},{224,192},{33,... | collective-permute-start | bytes 49160 | tf_op jit(solution)/shard_map/ppermute | solution.py:18
  237.8 8.1 %collective-permute-start.33 = (f32[8,2,1,256]{3,0,2,1:T(8,128)S(1)}, f32[8,2,1,256]{3,0,2,1:T(8,128)S(1)}, u32[]{:S(2)}, u32[]{:S(2)}) collective-permute-start(f32[8,2,1,256]{3,0,2,1:T(8,128)S(1)} %get-tuple-element.44), channel_id=1, source_target_pairs={{0,32},{32,64},{64,96},{96,128},{128,160},{160,192},{192,224},{1,3... | collective-permute-start | bytes 49160 | tf_op jit(solution)/shard_map/ppermute | solution.py:17
  249.7 7.0 collective-permute-start.34
  252.8 5.5 collective-permute-start.35
  267.0 8.2 %collective-permute-start.36 = (f32[8,2,1,256]{3,0,2,1:T(8,128)S(1)}, f32[8,2,1,256]{3,0,2,1:T(8,128)S(1)}, u32[]{:S(2)}, u32[]{:S(2)}) collective-permute-start(f32[8,2,1,256]{3,0,2,1:T(8,128)S(1)} %get-tuple-element.43), channel_id=1, source_target_pairs={{32,0},{64,32},{96,64},{128,96},{160,128},{192,160},{224,192},{33,... | collective-permute-start | bytes 49160 | tf_op jit(solution)/shard_map/ppermute | solution.py:18
  268.3 8.4 %collective-permute-start.37 = (f32[8,2,1,256]{3,0,2,1:T(8,128)S(1)}, f32[8,2,1,256]{3,0,2,1:T(8,128)S(1)}, u32[]{:S(2)}, u32[]{:S(2)}) collective-permute-start(f32[8,2,1,256]{3,0,2,1:T(8,128)S(1)} %get-tuple-element.42), channel_id=1, source_target_pairs={{0,32},{32,64},{64,96},{96,128},{128,160},{160,192},{192,224},{1,3... | collective-permute-start | bytes 49160 | tf_op jit(solution)/shard_map/ppermute | solution.py:17
  280.4 7.4 collective-permute-start.38
  283.8 5.7 collective-permute-start.39
  298.2 8.2 %collective-permute-start.40 = (f32[8,2,1,256]{3,0,2,1:T(8,128)S(1)}, f32[8,2,1,256]{3,0,2,1:T(8,128)S(1)}, u32[]{:S(2)}, u32[]{:S(2)}) collective-permute-start(f32[8,2,1,256]{3,0,2,1:T(8,128)S(1)} %get-tuple-element.41), channel_id=1, source_target_pairs={{32,0},{64,32},{96,64},{128,96},{160,128},{192,160},{224,192},{33,... | collective-permute-start | bytes 49160 | tf_op jit(solution)/shard_map/ppermute | solution.py:18
  299.5 8.4 %collective-permute-start.41 = (f32[8,2,1,256]{3,0,2,1:T(8,128)S(1)}, f32[8,2,1,256]{3,0,2,1:T(8,128)S(1)}, u32[]{:S(2)}, u32[]{:S(2)}) collective-permute-start(f32[8,2,1,256]{3,0,2,1:T(8,128)S(1)} %get-tuple-element.40), channel_id=1, source_target_pairs={{0,32},{32,64},{64,96},{96,128},{128,160},{160,192},{192,224},{1,3... | collective-permute-start | bytes 49160 | tf_op jit(solution)/shard_map/ppermute | solution.py:17
  310.1 16.6 %copy-start.20 = (f32[2,128,256]{2,1,0:T(8,128)S(1)}, f32[2,128,256]{2,1,0:T(8,128)}, u32[]{:S(2)}) copy-start(f32[2,128,256]{2,1,0:T(8,128)} %param.30) | copy-start | bytes 786436
  312.6 9.3 %collective-permute-start.42 = (f32[8,2,130,1]{2,0,3,1:T(8,128)}, f32[8,2,130,1]{2,0,3,1:T(8,128)}, u32[]{:S(2)}, u32[]{:S(2)}) collective-permute-start(f32[8,2,130,1]{2,0,3,1:T(8,128)} %copy.136), channel_id=1, source_target_pairs={{4,0},{8,4},{12,8},{16,12},{20,16},{24,20},{28,24},{5,1},{9,5},{13... | collective-permute-start | bytes 24968 | tf_op jit(solution)/shard_map/ppermute | solution.py:18
  316.4 7.9 %collective-permute-start.43 = (f32[8,2,130,1]{2,0,3,1:T(8,128)}, f32[8,2,130,1]{2,0,3,1:T(8,128)}, u32[]{:S(2)}, u32[]{:S(2)}) collective-permute-start(f32[8,2,130,1]{2,0,3,1:T(8,128)} %copy.138), channel_id=1, source_target_pairs={{0,4},{4,8},{8,12},{12,16},{16,20},{20,24},{24,28},{1,5},{5,9},{9,... | collective-permute-start | bytes 24968 | tf_op jit(solution)/shard_map/ppermute | solution.py:17
  (30 other events, 243.1 us)
Sparse Core Ops, SparseCore 0:
  335.1 99.3 all-gather.1
where the time goes:
time: 752 us; the launch traced here: 741 us
  blocking collectives  280 us (37%)
  starting transfers between devices  137 us (18%)
  waiting for transfers between devices  114 us (15%)
  local copies, waits for them, and re-layouts  103 us (14%)
  other arithmetic  81.4 us (11%)
  between operations  15.5 us (2%)
  matrix products  11 us (1%)
    psum x1, blocking collectives, on_device(): gram_sum = lax.psum(gram_local, ('gx', 'gy'))  280 us
    ppermute x22, starting transfers between devices, with_halo(): before = lax.ppermute(last, axis, up)  108 us
    all_gather x1, waiting for transfers between devices, on_device(): whole = lax.all_gather(own_flat, 'dir', axis=0, tiled=True)  99.5 us
    mul x8, other arithmetic, relax_sweep(): return ice_keep * (state + damping * (source - applied) / diagonal)  51.3 us
    slice x21, local copies, waits for them, and re-layouts, with_halo(): first = lax.slice_in_dim(value, 0, width, axis=dim)  37.7 us
    ppermute x22, starting transfers between devices, with_halo(): after = lax.ppermute(first, axis, down)  28.6 us
    slice x21, local copies, waits for them, and re-layouts, with_halo(): last = lax.slice_in_dim(value, length - width, length, axis=dim)  19.6 us
    ppermute x10, local copies, waits for them, and re-layouts, with_halo(): after = lax.ppermute(first, axis, down)  19.5 us
  transfers between devices with their start and end apart: 45, of which 11 were waited for; matrix products, arithmetic and copies ran while one was open for 6% of the time, Pallas kernels for 0%

commit v1 on v0

--- a/solution.py
+++ b/solution.py
@@ -82,7 +82,7 @@
     gram_local = jnp.dot(
         whole, whole.T, precision=lax.Precision.HIGHEST, preferred_element_type=jnp.float32
     )
-    gram_sum = lax.psum(gram_local, ("gx", "gy"))
+    gram_sum = lax.psum(lax.psum(gram_local, "gy"), "gx")
     lower = jnp.linalg.cholesky(gram_sum / jnp.float32(total_cells))
     inverse = lax.linalg.triangular_solve(lower, identity, left_side=True, lower=True)
     own_rows = lax.dynamic_slice_in_dim(inverse, lax.axis_index("dir") * own_count, own_count, 0)

time: 752 us -> 531 us (0.71)
  blocking collectives: 280 us -> 59.3 us
    psum x1 -> x2, blocking collectives: 280 us -> 59.3 us  [on_device(): gram_sum = lax.psum(lax.psum(gram_local, 'gy'), 'gx')]
  transfers between devices with their start and end apart: 45 -> 45, of which waited for: 11 -> 11; matrix products, arithmetic and copies ran while one was open for 6% -> 8% of each run, Pallas kernels for 0% -> 0%
where the time goes in v1:
time: 531 us; the launch traced here: 521 us
  starting transfers between devices  137 us (26%)
  waiting for transfers between devices  113 us (21%)
  local copies, waits for them, and re-layouts  103 us (19%)
  other arithmetic  81.7 us (15%)
  blocking collectives  59.3 us (11%)
  between operations  15.3 us (3%)
  matrix products  11 us (2%)
    ppermute x22, starting transfers between devices, with_halo(): before = lax.ppermute(last, axis, up)  108 us
    all_gather x1, waiting for transfers between devices, on_device(): whole = lax.all_gather(own_flat, 'dir', axis=0, tiled=True)  99.2 us
    psum x2, blocking collectives, on_device(): gram_sum = lax.psum(lax.psum(gram_local, 'gy'), 'gx')  59.3 us
    mul x8, other arithmetic, relax_sweep(): return ice_keep * (state + damping * (source - applied) / diagonal)  51.6 us
    slice x21, local copies, waits for them, and re-layouts, with_halo(): first = lax.slice_in_dim(value, 0, width, axis=dim)  37.6 us
    ppermute x22, starting transfers between devices, with_halo(): after = lax.ppermute(first, axis, down)  28.8 us
    slice x21, local copies, waits for them, and re-layouts, with_halo(): last = lax.slice_in_dim(value, length - width, length, axis=dim)  19.6 us
    ppermute x10, local copies, waits for them, and re-layouts, with_halo(): after = lax.ppermute(first, axis, down)  19.5 us
  transfers between devices with their start and end apart: 45, of which 11 were waited for; matrix products, arithmetic and copies ran while one was open for 8% of the time, Pallas kernels for 0%

profile of v1, /device:TPU:64, one launch (start us, length us, event | category | flops | bytes accessed | tf_op | source)
XLA Modules:
  0.0 520.5 jit_solution(9308581898606115700)
XLA Ops:
  9.3 4.5 collective-permute-start.1
  17.9 3.0 collective-permute-start.3
  25.3 4.5 collective-permute-start.5
  37.2 3.0 collective-permute-start.7
  44.2 7.6 %fusion.4 = f32[8,2,128,256]{3,0,2,1:T(8,128)S(1)} fusion(f32[8,2,128,256]{3,0,2,1:T(8,128)} %copy-done.8, f32[8,2,130,1]{3,0,2,1:T(8,128)} %copy.103, f32[8,2,1,256]{3,0,2,1:T(8,128)S(1)} %collective-permute-done.4, f32[8,2,1,256]{3,0,2,1:T(8,128)} %copy-done.25, f32[8,2,130,1]{3,0,2,1:T(8,128)} %copy.101, f32[128,256]{1,0:T(8,128)S(1)} %get-tuple-element.11, ...), kind=kLoop, calls=%fused_computation.20 | loop fusion | flops 15204352 | bytes 6603024 | tf_op jit(solution)/shard_map/mul | solution.py:41
  53.1 5.0 collective-permute-start.9
  61.8 2.5 copy.104
  65.5 2.5 copy.106
  68.0 4.8 collective-permute-start.11
  77.5 5.3 %fusion.8 = f32[8,2,128,256]{3,0,2,1:T(8,128)S(1)} fusion(f32[8,2,128,256]{3,0,2,1:T(8,128)S(1)} %fusion.4, f32[8,2,130,1]{3,0,2,1:T(8,128)} %copy.107, f32[8,2,1,256]{3,0,2,1:T(8,128)S(1)} %collective-permute-done.8, f32[8,2,1,256]{3,0,2,1:T(8,128)} %copy-done.26, f32[8,2,130,1]{3,0,2,1:T(8,128)} %copy.105, f32[128,256]{1,0:T(8,128)S(1)} %get-tuple-element.11, ...), kind=kLoop, calls=%fused_computation.24 | loop fusion | flops 15204352 | bytes 6603024 | tf_op jit(solution)/shard_map/mul | solution.py:41
  84.1 4.8 collective-permute-start.13
  92.6 2.6 copy.108
  96.5 2.5 copy.110
  99.0 3.8 collective-permute-start.15
  107.5 5.3 %fusion.12 = f32[8,2,128,256]{3,0,2,1:T(8,128)S(1)} fusion(f32[8,2,128,256]{3,0,2,1:T(8,128)S(1)} %copy-done.2, f32[8,2,130,1]{3,0,2,1:T(8,128)} %copy.111, f32[8,2,1,256]{3,0,2,1:T(8,128)S(1)} %collective-permute-done.12, f32[8,2,1,256]{3,0,2,1:T(8,128)} %copy-done.27, f32[8,2,130,1]{3,0,2,1:T(8,128)} %copy.109, f32[128,256]{1,0:T(8,128)S(1)} %get-tuple-element.11, ...), kind=kLoop, calls=%fused_computation.28 | loop fusion | flops 15204352 | bytes 6603024 | tf_op jit(solution)/shard_map/mul | solution.py:41
  114.1 6.7 %collective-permute-start.17 = (f32[8,2,1,256]{3,0,2,1:T(8,128)S(1)}, f32[8,2,1,256]{3,0,2,1:T(8,128)S(1)}, u32[]{:S(2)}, u32[]{:S(2)}) collective-permute-start(f32[8,2,1,256]{3,0,2,1:T(8,128)S(1)} %get-tuple-element.52), channel_id=1, source_target_pairs={{0,32},{32,64},{64,96},{96,128},{128,160},{160,192},{192,224},{1,3... | collective-permute-start | bytes 49160 | tf_op jit(solution)/shard_map/ppermute | solution.py:17
  124.5 2.6 copy.112
  128.4 2.5 copy.114
  130.9 3.6 collective-permute-start.19
  139.2 5.3 %fusion.16 = f32[8,2,128,256]{3,0,2,1:T(8,128)S(1)} fusion(f32[8,2,128,256]{3,0,2,1:T(8,128)S(1)} %copy-done.4, f32[8,2,130,1]{3,0,2,1:T(8,128)} %copy.115, f32[8,2,1,256]{3,0,2,1:T(8,128)S(1)} %collective-permute-done.16, f32[8,2,1,256]{3,0,2,1:T(8,128)} %copy-done.28, f32[8,2,130,1]{3,0,2,1:T(8,128)} %copy.113, f32[128,256]{1,0:T(8,128)S(1)} %get-tuple-element.11, ...), kind=kLoop, calls=%fused_computation.32 | loop fusion | flops 15204352 | bytes 6603024 | tf_op jit(solution)/shard_map/mul | solution.py:41
  145.8 6.9 %collective-permute-start.21 = (f32[8,2,1,256]{3,0,2,1:T(8,128)S(1)}, f32[8,2,1,256]{3,0,2,1:T(8,128)S(1)}, u32[]{:S(2)}, u32[]{:S(2)}) collective-permute-start(f32[8,2,1,256]{3,0,2,1:T(8,128)S(1)} %get-tuple-element.50), channel_id=1, source_target_pairs={{0,32},{32,64},{64,96},{96,128},{128,160},{160,192},{192,224},{1,3... | collective-permute-start | bytes 49160 | tf_op jit(solution)/shard_map/ppermute | solution.py:17
  160.1 3.0 collective-permute-start.23
  166.5 8.3 %multiply_divide_fusion = (f32[8,2,128,256]{3,0,2,1:T(8,128)S(1)}, f32[8,2,128,256]{3,0,2,1:T(8,128)S(1)}) fusion(f32[2,128,256]{2,1,0:T(8,128)S(1)} %get-tuple-element.69, f32[128,256]{1,0:T(8,128)} %copy-done.17, f32[8,2,128,256]{3,0,2,1:T(8,128)} %copy-done.9, f32[128,256]{1,0:T(8,128)S(1)} %get-tuple-element.11, ...), kind=kLoop, calls=%fused_computation.279 | loop fusion | flops 16777216 | bytes 8962320 | tf_op jit(solution)/shard_map/div | solution.py:46
  176.0 6.7 %collective-permute-start.25 = (f32[8,2,1,256]{3,0,2,1:T(8,128)S(1)}, f32[8,2,1,256]{3,0,2,1:T(8,128)S(1)}, u32[]{:S(2)}, u32[]{:S(2)}) collective-permute-start(f32[8,2,1,256]{3,0,2,1:T(8,128)S(1)} %get-tuple-element.48), channel_id=1, source_target_pairs={{0,32},{32,64},{64,96},{96,128},{128,160},{160,192},{192,224},{1,3... | collective-permute-start | bytes 49160 | tf_op jit(solution)/shard_map/ppermute | solution.py:17
  191.2 3.7 collective-permute-start.27
  198.2 7.3 %fusion.182 = f32[8,2,128,256]{3,0,2,1:T(8,128)S(1)} fusion(f32[8,2,128,256]{3,0,2,1:T(8,128)} %copy-done.10, f32[8,2,128,256]{3,0,2,1:T(8,128)S(1)} %get-tuple-element.13, f32[8,2,1,256]{3,0,2,1:T(8,128)S(1)} %collective-permute-done.24, f32[8,2,1,256]{3,0,2,1:T(8,128)S(1)} %collective-permute-done.25, f32[8,2,130,1]{3,0,2,1:T(8,128)} %copy.123, ...), kind=kLoop, calls=%fused_computation.280 | loop fusion | flops 14680064 | bytes 7389456 | tf_op jit(solution)/shard_map/mul | solution.py:41
  206.9 6.9 %collective-permute-start.29 = (f32[8,2,1,256]{3,0,2,1:T(8,128)S(1)}, f32[8,2,1,256]{3,0,2,1:T(8,128)S(1)}, u32[]{:S(2)}, u32[]{:S(2)}) collective-permute-start(f32[8,2,1,256]{3,0,2,1:T(8,128)S(1)} %get-tuple-element.46), channel_id=1, source_target_pairs={{0,32},{32,64},{64,96},{96,128},{128,160},{160,192},{192,224},{1,3... | collective-permute-start | bytes 49160 | tf_op jit(solution)/shard_map/ppermute | solution.py:17
  222.1 4.0 collective-permute-start.31
  229.5 7.0 %fusion.183 = f32[8,2,128,256]{3,0,2,1:T(8,128)S(1)} fusion(f32[8,2,128,256]{3,0,2,1:T(8,128)} %copy-done.5, f32[8,2,128,256]{3,0,2,1:T(8,128)S(1)} %get-tuple-element.13, f32[8,2,1,256]{3,0,2,1:T(8,128)S(1)} %collective-permute-done.28, f32[8,2,1,256]{3,0,2,1:T(8,128)S(1)} %collective-permute-done.29, f32[8,2,130,1]{3,0,2,1:T(8,128)} %copy.127, ...), kind=kLoop, calls=%fused_computation.281 | loop fusion | flops 14680064 | bytes 7389456 | tf_op jit(solution)/shard_map/mul | solution.py:41
  237.8 6.9 %collective-permute-start.33 = (f32[8,2,1,256]{3,0,2,1:T(8,128)S(1)}, f32[8,2,1,256]{3,0,2,1:T(8,128)S(1)}, u32[]{:S(2)}, u32[]{:S(2)}) collective-permute-start(f32[8,2,1,256]{3,0,2,1:T(8,128)S(1)} %get-tuple-element.44), channel_id=1, source_target_pairs={{0,32},{32,64},{64,96},{96,128},{128,160},{160,192},{192,224},{1,3... | collective-permute-start | bytes 49160 | tf_op jit(solution)/shard_map/ppermute | solution.py:17
  253.0 3.8 collective-permute-start.35
  260.1 7.0 %fusion.184 = f32[8,2,128,256]{3,0,2,1:T(8,128)S(1)} fusion(f32[8,2,128,256]{3,0,2,1:T(8,128)} %copy-done.6, f32[8,2,128,256]{3,0,2,1:T(8,128)S(1)} %get-tuple-element.13, f32[8,2,1,256]{3,0,2,1:T(8,128)S(1)} %collective-permute-done.32, f32[8,2,1,256]{3,0,2,1:T(8,128)S(1)} %collective-permute-done.33, f32[8,2,130,1]{3,0,2,1:T(8,128)} %copy.131, ...), kind=kLoop, calls=%fused_computation.282 | loop fusion | flops 14680064 | bytes 7389456 | tf_op jit(solution)/shard_map/mul | solution.py:41
  268.4 6.9 %collective-permute-start.37 = (f32[8,2,1,256]{3,0,2,1:T(8,128)S(1)}, f32[8,2,1,256]{3,0,2,1:T(8,128)S(1)}, u32[]{:S(2)}, u32[]{:S(2)}) collective-permute-start(f32[8,2,1,256]{3,0,2,1:T(8,128)S(1)} %get-tuple-element.42), channel_id=1, source_target_pairs={{0,32},{32,64},{64,96},{96,128},{128,160},{160,192},{192,224},{1,3... | collective-permute-start | bytes 49160 | tf_op jit(solution)/shard_map/ppermute | solution.py:17
  284.1 4.0 collective-permute-start.39
  291.4 7.0 %fusion.185 = f32[8,2,128,256]{3,0,2,1:T(8,128)S(1)} fusion(f32[8,2,128,256]{3,0,2,1:T(8,128)} %copy-done.7, f32[8,2,128,256]{3,0,2,1:T(8,128)S(1)} %get-tuple-element.13, f32[8,2,1,256]{3,0,2,1:T(8,128)S(1)} %collective-permute-done.36, f32[8,2,1,256]{3,0,2,1:T(8,128)S(1)} %collective-permute-done.37, f32[8,2,130,1]{3,0,2,1:T(8,128)} %copy.135, ...), kind=kLoop, calls=%fused_computation.283 | loop fusion | flops 14680064 | bytes 7389456 | tf_op jit(solution)/shard_map/mul | solution.py:41
  299.7 6.9 %collective-permute-start.41 = (f32[8,2,1,256]{3,0,2,1:T(8,128)S(1)}, f32[8,2,1,256]{3,0,2,1:T(8,128)S(1)}, u32[]{:S(2)}, u32[]{:S(2)}) collective-permute-start(f32[8,2,1,256]{3,0,2,1:T(8,128)S(1)} %get-tuple-element.40), channel_id=1, source_target_pairs={{0,32},{32,64},{64,96},{96,128},{128,160},{160,192},{192,224},{1,3... | collective-permute-start | bytes 49160 | tf_op jit(solution)/shard_map/ppermute | solution.py:17
  310.3 2.5 copy.136
  314.1 2.5 copy.138
  316.6 4.6 collective-permute-start.43
  324.6 2.4 copy.139
  327.0 7.1 %multiply_reduce_fusion = f32[8,128,256]{2,0,1:T(8,128)S(1)} fusion(f32[8,2,128,256]{3,0,2,1:T(8,128)} %copy-done, f32[8,2,128,256]{3,0,2,1:T(8,128)S(1)} %get-tuple-element.13, f32[8,2,1,256]{3,0,2,1:T(8,128)S(1)} %collective-permute-done.40, f32[8,2,1,256]{3,0,2,1:T(8,128)} %copy-done.23, f32[8,2,130,1]{3,0,2,1:T(8,128)} %copy.139, ...), kind=kLoop, calls=%fused_computation.278 | loop fusion | flops 15466496 | bytes 6603024 | tf_op jit(solution)/shard_map/reduce_sum | solution.py:76
  335.2 99.2 %all-gather.2.cloned.1.call-done = f32[32,32768]{1,0:T(8,128)} async-done(((f32[8,32768]{1,0:T(8,128)}), f32[32,32768]{1,0:T(8,128)}) %all-gather.2.cloned.1.call-update) | async-done | bytes 4194320 | tf_op jit(solution)/shard_map/all_gather | solution.py:81
  434.4 7.0 %fusion.230 = f32[32,32]{0,1:T(8,128)S(1)} fusion(f32[32,32768]{1,0:T(8,128)} %all-gather.2.cloned.1.call-done), kind=kOutput, calls=%fused_computation.346 | convolution fusion | flops 402653184 | bytes 4198400 | tf_op jit(solution)/shard_map/dot_general | solution.py:82
  441.4 23.6 %psum.14 = f32[32,32]{0,1:T(8,128)S(1)} all-reduce(f32[32,32]{0,1:T(8,128)S(1)} %fusion.230), channel_id=1, replica_groups=mesh['gx'=8,'gy'=8,'dir'=4] {'gy'}, use_global_device_ids=true, to_apply=%region_1.0 | all-reduce | flops 1024 | bytes 8192 | tf_op jit(solution)/shard_map/psum | solution.py:85
  464.9 35.7 %psum.15 = f32[32,32]{0,1:T(8,128)S(1)} all-reduce(f32[32,32]{0,1:T(8,128)S(1)} %psum.14), channel_id=1, replica_groups=mesh['gx'=8,'gy'=8,'dir'=4] {'gx'}, use_global_device_ids=true, to_apply=%region_2.0 | all-reduce | flops 1024 | bytes 8192 | tf_op jit(solution)/shard_map/psum | solution.py:85
  500.8 2.9 cholesky.17
  505.0 2.4 custom-call.6
  507.7 3.8 fusion.198
  (217 shorter events, 132.8 us)
Async XLA Ops:
  7.2 15.4 %copy-start.21 = (f32[128,256]{1,0:T(8,128)S(1)}, f32[128,256]{1,0:T(8,128)}, u32[]{:S(2)}) copy-start(f32[128,256]{1,0:T(8,128)} %param.31) | copy-start | bytes 393220
  7.2 427.2 %all-gather.2.cloned.1.call-start = ((), (), s32[]{:S(2)}) async-start(), calls=%async_computation | async-start | bytes 5242880 | tf_op jit(solution)/shard_map/all_gather | solution.py:81
  8.0 7.5 %collective-permute-start = (f32[1,256]{1,0:T(1,128)S(1)}, f32[1,256]{1,0:T(1,128)S(1)}, u32[]{:S(2)}, u32[]{:S(2)}) collective-permute-start(f32[1,256]{1,0:T(1,128)S(1)} %get-tuple-element.66), channel_id=1, source_target_pairs={{32,0},{64,32},{96,64},{128,96},{160,128},{192,160},{224,192},{33,... | collective-permute-start | bytes 3080 | tf_op jit(solution)/shard_map/ppermute | solution.py:18
  9.3 6.2 %collective-permute-start.1 = (f32[1,256]{1,0:T(1,128)S(1)}, f32[1,256]{1,0:T(1,128)S(1)}, u32[]{:S(2)}, u32[]{:S(2)}) collective-permute-start(f32[1,256]{1,0:T(1,128)S(1)} %get-tuple-element.65), channel_id=1, source_target_pairs={{0,32},{32,64},{64,96},{96,128},{128,160},{160,192},{192,224},{1,3... | collective-permute-start | bytes 3080 | tf_op jit(solution)/shard_map/ppermute | solution.py:17
  16.6 5.9 %collective-permute-start.2 = (f32[130,1]{1,0:T(8,128)S(1)}, f32[130,1]{1,0:T(8,128)S(1)}, u32[]{:S(2)}, u32[]{:S(2)}) collective-permute-start(f32[130,1]{1,0:T(8,128)S(1)} %get-tuple-element.60), channel_id=1, source_target_pairs={{4,0},{8,4},{12,8},{16,12},{20,16},{24,20},{28,24},{5,1},{9,5},{13... | collective-permute-start | bytes 1568 | tf_op jit(solution)/shard_map/ppermute | solution.py:18
  17.9 4.6 collective-permute-start.3
  24.0 5.9 %collective-permute-start.4 = (f32[8,2,1,256]{3,0,2,1:T(8,128)S(1)}, f32[8,2,1,256]{3,0,2,1:T(8,128)S(1)}, u32[]{:S(2)}, u32[]{:S(2)}) collective-permute-start(f32[8,2,1,256]{3,0,2,1:T(8,128)S(1)} %get-tuple-element.59), channel_id=1, source_target_pairs={{32,0},{64,32},{96,64},{128,96},{160,128},{192,160},{224,192},{33,... | collective-permute-start | bytes 49160 | tf_op jit(solution)/shard_map/ppermute | solution.py:18
  25.3 6.0 %collective-permute-start.5 = (f32[8,2,1,256]{3,0,2,1:T(8,128)S(1)}, f32[8,2,1,256]{3,0,2,1:T(8,128)S(1)}, u32[]{:S(2)}, u32[]{:S(2)}) collective-permute-start(f32[8,2,1,256]{3,0,2,1:T(8,128)S(1)} %get-tuple-element.58), channel_id=1, source_target_pairs={{0,32},{32,64},{64,96},{96,128},{128,160},{160,192},{192,224},{1,3... | collective-permute-start | bytes 49160 | tf_op jit(solution)/shard_map/ppermute | solution.py:17
  35.2 5.7 %collective-permute-start.6 = (f32[8,2,130,1]{2,0,3,1:T(8,128)S(1)}, f32[8,2,130,1]{2,0,3,1:T(8,128)S(1)}, u32[]{:S(2)}, u32[]{:S(2)}) collective-permute-start(f32[8,2,130,1]{2,0,3,1:T(8,128)S(1)} %copy.100), channel_id=1, source_target_pairs={{4,0},{8,4},{12,8},{16,12},{20,16},{24,20},{28,24},{5,1},{9,5},{13... | collective-permute-start | bytes 24968 | tf_op jit(solution)/shard_map/ppermute | solution.py:18
  37.2 5.4 %collective-permute-start.7 = (f32[8,2,130,1]{2,0,3,1:T(8,128)S(1)}, f32[8,2,130,1]{2,0,3,1:T(8,128)S(1)}, u32[]{:S(2)}, u32[]{:S(2)}) collective-permute-start(f32[8,2,130,1]{2,0,3,1:T(8,128)S(1)} %copy.102), channel_id=1, source_target_pairs={{0,4},{4,8},{8,12},{12,16},{16,20},{20,24},{24,28},{1,5},{5,9},{9,... | collective-permute-start | bytes 24968 | tf_op jit(solution)/shard_map/ppermute | solution.py:17
  51.8 6.3 %collective-permute-start.8 = (f32[8,2,1,256]{3,0,2,1:T(8,128)S(1)}, f32[8,2,1,256]{3,0,2,1:T(8,128)S(1)}, u32[]{:S(2)}, u32[]{:S(2)}) collective-permute-start(f32[8,2,1,256]{3,0,2,1:T(8,128)S(1)} %get-tuple-element.57), channel_id=1, source_target_pairs={{32,0},{64,32},{96,64},{128,96},{160,128},{192,160},{224,192},{33,... | collective-permute-start | bytes 49160 | tf_op jit(solution)/shard_map/ppermute | solution.py:18
  53.1 6.4 %collective-permute-start.9 = (f32[8,2,1,256]{3,0,2,1:T(8,128)S(1)}, f32[8,2,1,256]{3,0,2,1:T(8,128)S(1)}, u32[]{:S(2)}, u32[]{:S(2)}) collective-permute-start(f32[8,2,1,256]{3,0,2,1:T(8,128)S(1)} %get-tuple-element.56), channel_id=1, source_target_pairs={{0,32},{32,64},{64,96},{96,128},{128,160},{160,192},{192,224},{1,3... | collective-permute-start | bytes 49160 | tf_op jit(solution)/shard_map/ppermute | solution.py:17
  64.2 8.6 %collective-permute-start.10 = (f32[8,2,130,1]{2,0,3,1:T(8,128)}, f32[8,2,130,1]{2,0,3,1:T(8,128)}, u32[]{:S(2)}, u32[]{:S(2)}) collective-permute-start(f32[8,2,130,1]{2,0,3,1:T(8,128)} %copy.104), channel_id=1, source_target_pairs={{4,0},{8,4},{12,8},{16,12},{20,16},{24,20},{28,24},{5,1},{9,5},{13... | collective-permute-start | bytes 24968 | tf_op jit(solution)/shard_map/ppermute | solution.py:18
  68.0 7.2 %collective-permute-start.11 = (f32[8,2,130,1]{2,0,3,1:T(8,128)}, f32[8,2,130,1]{2,0,3,1:T(8,128)}, u32[]{:S(2)}, u32[]{:S(2)}) collective-permute-start(f32[8,2,130,1]{2,0,3,1:T(8,128)} %copy.106), channel_id=1, source_target_pairs={{0,4},{4,8},{8,12},{12,16},{16,20},{20,24},{24,28},{1,5},{5,9},{9,... | collective-permute-start | bytes 24968 | tf_op jit(solution)/shard_map/ppermute | solution.py:17
  82.8 6.1 %collective-permute-start.12 = (f32[8,2,1,256]{3,0,2,1:T(8,128)S(1)}, f32[8,2,1,256]{3,0,2,1:T(8,128)S(1)}, u32[]{:S(2)}, u32[]{:S(2)}) collective-permute-start(f32[8,2,1,256]{3,0,2,1:T(8,128)S(1)} %get-tuple-element.55), channel_id=1, source_target_pairs={{32,0},{64,32},{96,64},{128,96},{160,128},{192,160},{224,192},{33,... | collective-permute-start | bytes 49160 | tf_op jit(solution)/shard_map/ppermute | solution.py:18
  84.1 6.2 %collective-permute-start.13 = (f32[8,2,1,256]{3,0,2,1:T(8,128)S(1)}, f32[8,2,1,256]{3,0,2,1:T(8,128)S(1)}, u32[]{:S(2)}, u32[]{:S(2)}) collective-permute-start(f32[8,2,1,256]{3,0,2,1:T(8,128)S(1)} %get-tuple-element.54), channel_id=1, source_target_pairs={{0,32},{32,64},{64,96},{96,128},{128,160},{160,192},{192,224},{1,3... | collective-permute-start | bytes 49160 | tf_op jit(solution)/shard_map/ppermute | solution.py:17
  92.6 14.9 %copy-start.2 = (f32[8,2,128,256]{3,0,2,1:T(8,128)S(1)}, f32[8,2,128,256]{3,0,2,1:T(8,128)}, u32[]{:S(2)}) copy-start(f32[8,2,128,256]{3,0,2,1:T(8,128)} %copy-done.1) | copy-start | bytes 6291460
  95.2 7.5 %collective-permute-start.14 = (f32[8,2,130,1]{2,0,3,1:T(8,128)}, f32[8,2,130,1]{2,0,3,1:T(8,128)}, u32[]{:S(2)}, u32[]{:S(2)}) collective-permute-start(f32[8,2,130,1]{2,0,3,1:T(8,128)} %copy.108), channel_id=1, source_target_pairs={{4,0},{8,4},{12,8},{16,12},{20,16},{24,20},{28,24},{5,1},{9,5},{13... | collective-permute-start | bytes 24968 | tf_op jit(solution)/shard_map/ppermute | solution.py:18
  99.0 6.2 %collective-permute-start.15 = (f32[8,2,130,1]{2,0,3,1:T(8,128)}, f32[8,2,130,1]{2,0,3,1:T(8,128)}, u32[]{:S(2)}, u32[]{:S(2)}) collective-permute-start(f32[8,2,130,1]{2,0,3,1:T(8,128)} %copy.110), channel_id=1, source_target_pairs={{0,4},{4,8},{8,12},{12,16},{16,20},{20,24},{24,28},{1,5},{5,9},{9,... | collective-permute-start | bytes 24968 | tf_op jit(solution)/shard_map/ppermute | solution.py:17
  112.8 8.0 %collective-permute-start.16 = (f32[8,2,1,256]{3,0,2,1:T(8,128)S(1)}, f32[8,2,1,256]{3,0,2,1:T(8,128)S(1)}, u32[]{:S(2)}, u32[]{:S(2)}) collective-permute-start(f32[8,2,1,256]{3,0,2,1:T(8,128)S(1)} %get-tuple-element.53), channel_id=1, source_target_pairs={{32,0},{64,32},{96,64},{128,96},{160,128},{192,160},{224,192},{33,... | collective-permute-start | bytes 49160 | tf_op jit(solution)/shard_map/ppermute | solution.py:18
  114.1 8.1 %collective-permute-start.17 = (f32[8,2,1,256]{3,0,2,1:T(8,128)S(1)}, f32[8,2,1,256]{3,0,2,1:T(8,128)S(1)}, u32[]{:S(2)}, u32[]{:S(2)}) collective-permute-start(f32[8,2,1,256]{3,0,2,1:T(8,128)S(1)} %get-tuple-element.52), channel_id=1, source_target_pairs={{0,32},{32,64},{64,96},{96,128},{128,160},{160,192},{192,224},{1,3... | collective-permute-start | bytes 49160 | tf_op jit(solution)/shard_map/ppermute | solution.py:17
  127.1 7.4 %collective-permute-start.18 = (f32[8,2,130,1]{2,0,3,1:T(8,128)}, f32[8,2,130,1]{2,0,3,1:T(8,128)}, u32[]{:S(2)}, u32[]{:S(2)}) collective-permute-start(f32[8,2,130,1]{2,0,3,1:T(8,128)} %copy.112), channel_id=1, source_target_pairs={{4,0},{8,4},{12,8},{16,12},{20,16},{24,20},{28,24},{5,1},{9,5},{13... | collective-permute-start | bytes 24968 | tf_op jit(solution)/shard_map/ppermute | solution.py:18
  130.9 6.0 %collective-permute-start.19 = (f32[8,2,130,1]{2,0,3,1:T(8,128)}, f32[8,2,130,1]{2,0,3,1:T(8,128)}, u32[]{:S(2)}, u32[]{:S(2)}) collective-permute-start(f32[8,2,130,1]{2,0,3,1:T(8,128)} %copy.114), channel_id=1, source_target_pairs={{0,4},{4,8},{8,12},{12,16},{16,20},{20,24},{24,28},{1,5},{5,9},{9,... | collective-permute-start | bytes 24968 | tf_op jit(solution)/shard_map/ppermute | solution.py:17
  144.6 8.2 %collective-permute-start.20 = (f32[8,2,1,256]{3,0,2,1:T(8,128)S(1)}, f32[8,2,1,256]{3,0,2,1:T(8,128)S(1)}, u32[]{:S(2)}, u32[]{:S(2)}) collective-permute-start(f32[8,2,1,256]{3,0,2,1:T(8,128)S(1)} %get-tuple-element.51), channel_id=1, source_target_pairs={{32,0},{64,32},{96,64},{128,96},{160,128},{192,160},{224,192},{33,... | collective-permute-start | bytes 49160 | tf_op jit(solution)/shard_map/ppermute | solution.py:18
  145.8 8.4 %collective-permute-start.21 = (f32[8,2,1,256]{3,0,2,1:T(8,128)S(1)}, f32[8,2,1,256]{3,0,2,1:T(8,128)S(1)}, u32[]{:S(2)}, u32[]{:S(2)}) collective-permute-start(f32[8,2,1,256]{3,0,2,1:T(8,128)S(1)} %get-tuple-element.50), channel_id=1, source_target_pairs={{0,32},{32,64},{64,96},{96,128},{128,160},{160,192},{192,224},{1,3... | collective-permute-start | bytes 49160 | tf_op jit(solution)/shard_map/ppermute | solution.py:17
  158.2 5.0 collective-permute-start.22
  160.1 4.7 collective-permute-start.23
  174.7 8.0 %collective-permute-start.24 = (f32[8,2,1,256]{3,0,2,1:T(8,128)S(1)}, f32[8,2,1,256]{3,0,2,1:T(8,128)S(1)}, u32[]{:S(2)}, u32[]{:S(2)}) collective-permute-start(f32[8,2,1,256]{3,0,2,1:T(8,128)S(1)} %get-tuple-element.49), channel_id=1, source_target_pairs={{32,0},{64,32},{96,64},{128,96},{160,128},{192,160},{224,192},{33,... | collective-permute-start | bytes 49160 | tf_op jit(solution)/shard_map/ppermute | solution.py:18
  176.0 8.1 %collective-permute-start.25 = (f32[8,2,1,256]{3,0,2,1:T(8,128)S(1)}, f32[8,2,1,256]{3,0,2,1:T(8,128)S(1)}, u32[]{:S(2)}, u32[]{:S(2)}) collective-permute-start(f32[8,2,1,256]{3,0,2,1:T(8,128)S(1)} %get-tuple-element.48), channel_id=1, source_target_pairs={{0,32},{32,64},{64,96},{96,128},{128,160},{160,192},{192,224},{1,3... | collective-permute-start | bytes 49160 | tf_op jit(solution)/shard_map/ppermute | solution.py:17
  188.0 6.8 %collective-permute-start.26 = (f32[8,2,130,1]{2,0,3,1:T(8,128)S(1)}, f32[8,2,130,1]{2,0,3,1:T(8,128)S(1)}, u32[]{:S(2)}, u32[]{:S(2)}) collective-permute-start(f32[8,2,130,1]{2,0,3,1:T(8,128)S(1)} %copy.120), channel_id=1, source_target_pairs={{4,0},{8,4},{12,8},{16,12},{20,16},{24,20},{28,24},{5,1},{9,5},{13... | collective-permute-start | bytes 24968 | tf_op jit(solution)/shard_map/ppermute | solution.py:18
  191.2 5.4 %collective-permute-start.27 = (f32[8,2,130,1]{2,0,3,1:T(8,128)S(1)}, f32[8,2,130,1]{2,0,3,1:T(8,128)S(1)}, u32[]{:S(2)}, u32[]{:S(2)}) collective-permute-start(f32[8,2,130,1]{2,0,3,1:T(8,128)S(1)} %copy.122), channel_id=1, source_target_pairs={{0,4},{4,8},{8,12},{12,16},{16,20},{20,24},{24,28},{1,5},{5,9},{9,... | collective-permute-start | bytes 24968 | tf_op jit(solution)/shard_map/ppermute | solution.py:17
  205.6 8.2 %collective-permute-start.28 = (f32[8,2,1,256]{3,0,2,1:T(8,128)S(1)}, f32[8,2,1,256]{3,0,2,1:T(8,128)S(1)}, u32[]{:S(2)}, u32[]{:S(2)}) collective-permute-start(f32[8,2,1,256]{3,0,2,1:T(8,128)S(1)} %get-tuple-element.47), channel_id=1, source_target_pairs={{32,0},{64,32},{96,64},{128,96},{160,128},{192,160},{224,192},{33,... | collective-permute-start | bytes 49160 | tf_op jit(solution)/shard_map/ppermute | solution.py:18
  206.9 8.4 %collective-permute-start.29 = (f32[8,2,1,256]{3,0,2,1:T(8,128)S(1)}, f32[8,2,1,256]{3,0,2,1:T(8,128)S(1)}, u32[]{:S(2)}, u32[]{:S(2)}) collective-permute-start(f32[8,2,1,256]{3,0,2,1:T(8,128)S(1)} %get-tuple-element.46), channel_id=1, source_target_pairs={{0,32},{32,64},{64,96},{96,128},{128,160},{160,192},{192,224},{1,3... | collective-permute-start | bytes 49160 | tf_op jit(solution)/shard_map/ppermute | solution.py:17
  219.0 7.2 %collective-permute-start.30 = (f32[8,2,130,1]{2,0,3,1:T(8,128)S(1)}, f32[8,2,130,1]{2,0,3,1:T(8,128)S(1)}, u32[]{:S(2)}, u32[]{:S(2)}) collective-permute-start(f32[8,2,130,1]{2,0,3,1:T(8,128)S(1)} %copy.124), channel_id=1, source_target_pairs={{4,0},{8,4},{12,8},{16,12},{20,16},{24,20},{28,24},{5,1},{9,5},{13... | collective-permute-start | bytes 24968 | tf_op jit(solution)/shard_map/ppermute | solution.py:18
  222.1 5.7 %collective-permute-start.31 = (f32[8,2,130,1]{2,0,3,1:T(8,128)S(1)}, f32[8,2,130,1]{2,0,3,1:T(8,128)S(1)}, u32[]{:S(2)}, u32[]{:S(2)}) collective-permute-start(f32[8,2,130,1]{2,0,3,1:T(8,128)S(1)} %copy.126), channel_id=1, source_target_pairs={{0,4},{4,8},{8,12},{12,16},{16,20},{20,24},{24,28},{1,5},{5,9},{9,... | collective-permute-start | bytes 24968 | tf_op jit(solution)/shard_map/ppermute | solution.py:17
  236.5 8.2 %collective-permute-start.32 = (f32[8,2,1,256]{3,0,2,1:T(8,128)S(1)}, f32[8,2,1,256]{3,0,2,1:T(8,128)S(1)}, u32[]{:S(2)}, u32[]{:S(2)}) collective-permute-start(f32[8,2,1,256]{3,0,2,1:T(8,128)S(1)} %get-tuple-element.45), channel_id=1, source_target_pairs={{32,0},{64,32},{96,64},{128,96},{160,128},{192,160},{224,192},{33,... | collective-permute-start | bytes 49160 | tf_op jit(solution)/shard_map/ppermute | solution.py:18
  237.8 8.4 %collective-permute-start.33 = (f32[8,2,1,256]{3,0,2,1:T(8,128)S(1)}, f32[8,2,1,256]{3,0,2,1:T(8,128)S(1)}, u32[]{:S(2)}, u32[]{:S(2)}) collective-permute-start(f32[8,2,1,256]{3,0,2,1:T(8,128)S(1)} %get-tuple-element.44), channel_id=1, source_target_pairs={{0,32},{32,64},{64,96},{96,128},{128,160},{160,192},{192,224},{1,3... | collective-permute-start | bytes 49160 | tf_op jit(solution)/shard_map/ppermute | solution.py:17
  249.8 7.0 %collective-permute-start.34 = (f32[8,2,130,1]{2,0,3,1:T(8,128)S(1)}, f32[8,2,130,1]{2,0,3,1:T(8,128)S(1)}, u32[]{:S(2)}, u32[]{:S(2)}) collective-permute-start(f32[8,2,130,1]{2,0,3,1:T(8,128)S(1)} %copy.128), channel_id=1, source_target_pairs={{4,0},{8,4},{12,8},{16,12},{20,16},{24,20},{28,24},{5,1},{9,5},{13... | collective-permute-start | bytes 24968 | tf_op jit(solution)/shard_map/ppermute | solution.py:18
  253.0 5.5 %collective-permute-start.35 = (f32[8,2,130,1]{2,0,3,1:T(8,128)S(1)}, f32[8,2,130,1]{2,0,3,1:T(8,128)S(1)}, u32[]{:S(2)}, u32[]{:S(2)}) collective-permute-start(f32[8,2,130,1]{2,0,3,1:T(8,128)S(1)} %copy.130), channel_id=1, source_target_pairs={{0,4},{4,8},{8,12},{12,16},{16,20},{20,24},{24,28},{1,5},{5,9},{9,... | collective-permute-start | bytes 24968 | tf_op jit(solution)/shard_map/ppermute | solution.py:17
  267.1 8.2 %collective-permute-start.36 = (f32[8,2,1,256]{3,0,2,1:T(8,128)S(1)}, f32[8,2,1,256]{3,0,2,1:T(8,128)S(1)}, u32[]{:S(2)}, u32[]{:S(2)}) collective-permute-start(f32[8,2,1,256]{3,0,2,1:T(8,128)S(1)} %get-tuple-element.43), channel_id=1, source_target_pairs={{32,0},{64,32},{96,64},{128,96},{160,128},{192,160},{224,192},{33,... | collective-permute-start | bytes 49160 | tf_op jit(solution)/shard_map/ppermute | solution.py:18
  268.4 8.4 %collective-permute-start.37 = (f32[8,2,1,256]{3,0,2,1:T(8,128)S(1)}, f32[8,2,1,256]{3,0,2,1:T(8,128)S(1)}, u32[]{:S(2)}, u32[]{:S(2)}) collective-permute-start(f32[8,2,1,256]{3,0,2,1:T(8,128)S(1)} %get-tuple-element.42), channel_id=1, source_target_pairs={{0,32},{32,64},{64,96},{96,128},{128,160},{160,192},{192,224},{1,3... | collective-permute-start | bytes 49160 | tf_op jit(solution)/shard_map/ppermute | solution.py:17
  280.5 7.6 %collective-permute-start.38 = (f32[8,2,130,1]{2,0,3,1:T(8,128)S(1)}, f32[8,2,130,1]{2,0,3,1:T(8,128)S(1)}, u32[]{:S(2)}, u32[]{:S(2)}) collective-permute-start(f32[8,2,130,1]{2,0,3,1:T(8,128)S(1)} %copy.132), channel_id=1, source_target_pairs={{4,0},{8,4},{12,8},{16,12},{20,16},{24,20},{28,24},{5,1},{9,5},{13... | collective-permute-start | bytes 24968 | tf_op jit(solution)/shard_map/ppermute | solution.py:18
  284.1 5.7 %collective-permute-start.39 = (f32[8,2,130,1]{2,0,3,1:T(8,128)S(1)}, f32[8,2,130,1]{2,0,3,1:T(8,128)S(1)}, u32[]{:S(2)}, u32[]{:S(2)}) collective-permute-start(f32[8,2,130,1]{2,0,3,1:T(8,128)S(1)} %copy.134), channel_id=1, source_target_pairs={{0,4},{4,8},{8,12},{12,16},{16,20},{20,24},{24,28},{1,5},{5,9},{9,... | collective-permute-start | bytes 24968 | tf_op jit(solution)/shard_map/ppermute | solution.py:17
  298.4 8.2 %collective-permute-start.40 = (f32[8,2,1,256]{3,0,2,1:T(8,128)S(1)}, f32[8,2,1,256]{3,0,2,1:T(8,128)S(1)}, u32[]{:S(2)}, u32[]{:S(2)}) collective-permute-start(f32[8,2,1,256]{3,0,2,1:T(8,128)S(1)} %get-tuple-element.41), channel_id=1, source_target_pairs={{32,0},{64,32},{96,64},{128,96},{160,128},{192,160},{224,192},{33,... | collective-permute-start | bytes 49160 | tf_op jit(solution)/shard_map/ppermute | solution.py:18
  299.7 8.4 %collective-permute-start.41 = (f32[8,2,1,256]{3,0,2,1:T(8,128)S(1)}, f32[8,2,1,256]{3,0,2,1:T(8,128)S(1)}, u32[]{:S(2)}, u32[]{:S(2)}) collective-permute-start(f32[8,2,1,256]{3,0,2,1:T(8,128)S(1)} %get-tuple-element.40), channel_id=1, source_target_pairs={{0,32},{32,64},{64,96},{96,128},{128,160},{160,192},{192,224},{1,3... | collective-permute-start | bytes 49160 | tf_op jit(solution)/shard_map/ppermute | solution.py:17
  310.3 16.6 %copy-start.20 = (f32[2,128,256]{2,1,0:T(8,128)S(1)}, f32[2,128,256]{2,1,0:T(8,128)}, u32[]{:S(2)}) copy-start(f32[2,128,256]{2,1,0:T(8,128)} %param.30) | copy-start | bytes 786436
  312.8 9.3 %collective-permute-start.42 = (f32[8,2,130,1]{2,0,3,1:T(8,128)}, f32[8,2,130,1]{2,0,3,1:T(8,128)}, u32[]{:S(2)}, u32[]{:S(2)}) collective-permute-start(f32[8,2,130,1]{2,0,3,1:T(8,128)} %copy.136), channel_id=1, source_target_pairs={{4,0},{8,4},{12,8},{16,12},{20,16},{24,20},{28,24},{5,1},{9,5},{13... | collective-permute-start | bytes 24968 | tf_op jit(solution)/shard_map/ppermute | solution.py:18
  316.6 7.9 %collective-permute-start.43 = (f32[8,2,130,1]{2,0,3,1:T(8,128)}, f32[8,2,130,1]{2,0,3,1:T(8,128)}, u32[]{:S(2)}, u32[]{:S(2)}) collective-permute-start(f32[8,2,130,1]{2,0,3,1:T(8,128)} %copy.138), channel_id=1, source_target_pairs={{0,4},{4,8},{8,12},{12,16},{16,20},{20,24},{24,28},{1,5},{5,9},{9,... | collective-permute-start | bytes 24968 | tf_op jit(solution)/shard_map/ppermute | solution.py:17
  (30 other events, 243.7 us)
Sparse Core Ops, SparseCore 0:
  335.3 99.0 all-gather.1
